TPU v7x, 32 devices: a whole 2x2x4 slice. The times are simulated.
32 devices in a mesh: surf: 8 (over z, x), col: 4 (over y, core).
Axes of the slice: x: 2, y: 2, z: 4, core: 2. Of those that a mesh axis runs over, the one named last changes fastest.
Arguments:
- stiffness: float32 [32, 3, 512, 512], P(('surf', 'col'))
- load: float32 [32, 3, 512, 256], P(('surf', 'col')), may hold values from -6 to 6
- start: float32 [32, 3, 512, 256], P(('surf', 'col')), may hold values from -6 to 6
- boundary_matrix: float32 [512, 4, 2048], P('surf', None, 'col'), may hold values from -0.125 to 0.125
- bem_node: int32 [4, 512], P('col'), may hold values from 0 to 511, as said below
Outputs:
- solution_field: float32 [32, 3, 512, 256], P(('surf', 'col'))
- traction: float32 [4, 512, 256], P('col', 'surf')
Inputs may be any that keep to these rules, and one draw needn't show every extreme that they name: Each row bem_node[g] is a permutation of 0 to 512 - 1 (the top face nodes of column group g). For each block of 64 slots q in [s * 64, (s + 1) * 64) and each patch s2 of the group, the block's slots name either exactly 8 node of patch s2 or none; each patch's top face nodes lie in exactly 8 blocks.
All inputs are finite; a program needn't handle non-finite values.
Results may differ from a plain program's by a relative error of at most 0.0001.
Values sent between devices are 32-bit elements; how exact they have to be, the bound alone decides.
No kernel may reach another device: no remote copies, remote signals or barrier semaphores. Data moves between devices by JAX's collectives and lax.ppermute only.
A program may use at most 128 MiB of HBM per device.

v0:
```python
import jax
import jax.numpy as jnp
from jax import lax
from jax.sharding import PartitionSpec as P

EDGE = 8
ITERS = 2
damping = 0.25
coupling = 0.5


def with_halo(block, sides, width):
    for axis, dim in sides:
        count = lax.axis_size(axis)
        forward = [(i, i + 1) for i in range(count - 1)]
        backward = [(target, source) for source, target in forward]
        low = lax.ppermute(
            lax.slice_in_dim(block, block.shape[dim] - width, None, axis=dim), axis, forward
        )
        high = lax.ppermute(lax.slice_in_dim(block, 0, width, axis=dim), axis, backward)
        block = jnp.concatenate([low, block, high], axis=dim)
    return block


def volume_apply(current, kmats, edge_cells, layers_deep, fields):
    highest = lax.Precision.HIGHEST
    cube = current.reshape(layers_deep, edge_cells, edge_cells, edge_cells, fields)
    padded = with_halo(cube, (("surf", 1), ("col", 2)), 1)
    extra = jnp.zeros_like(cube)
    extra = extra.at[:, 0].add(cube[:, 0] - padded[:, 0, 1:-1])
    extra = extra.at[:, -1].add(cube[:, -1] - padded[:, -1, 1:-1])
    extra = extra.at[:, :, 0].add(cube[:, :, 0] - padded[:, 1:-1, 0])
    extra = extra.at[:, :, -1].add(cube[:, :, -1] - padded[:, 1:-1, -1])
    low_k = cube[:, :, :, 0]
    high_k = cube[:, :, :, -1]
    deeper = jnp.concatenate([low_k[1:], jnp.zeros_like(low_k[:1])], axis=0)
    extra = extra.at[:, :, :, -1].add(high_k - deeper)
    extra = extra.at[1:, :, :, 0].add(low_k[1:] - high_k[:-1])
    applied = jnp.einsum("dab,dbf->daf", kmats, current, precision=highest)
    return applied.reshape(cube.shape) + coupling * extra


def rank_within(labels_row, order_key):
    same_label = labels_row[:, None] == labels_row[None, :]
    earlier = order_key[None, :] < order_key[:, None]
    return jnp.sum(jnp.logical_and(same_label, earlier), axis=1)


def shards(stiffness, load, start, boundary_matrix, bem_node):
    highest = lax.Precision.HIGHEST
    surf_count = lax.axis_size("surf")
    my_index = lax.axis_index("surf")
    layers_deep = stiffness.shape[1]
    node_count = stiffness.shape[2]
    fields = load.shape[3]
    edge_cells = EDGE
    face_nodes = edge_cells * edge_cells
    per_pair = max(face_nodes // surf_count, 1)
    group_map = bem_node[0]
    group_size = group_map.shape[0]
    slot_of_node = jnp.argsort(group_map)
    kmats = stiffness[0]
    load_cube = load[0].reshape(layers_deep, edge_cells, edge_cells, edge_cells, fields)
    operator_rows = boundary_matrix.reshape(-1, group_size)
    local_order = jnp.arange(face_nodes, dtype=jnp.int32)
    my_block_nodes = lax.dynamic_slice_in_dim(group_map, my_index * face_nodes, face_nodes)
    block_owners = my_block_nodes // face_nodes
    block_local = my_block_nodes % face_nodes
    slot_index = block_owners * per_pair + rank_within(block_owners, block_local)
    my_node_slots = lax.dynamic_slice_in_dim(slot_of_node, my_index * face_nodes, face_nodes)
    node_holders = my_node_slots // face_nodes
    send_index = node_holders * per_pair + rank_within(node_holders, local_order)
    current = start[0]
    traction_rows = jnp.zeros((face_nodes, fields), jnp.float32)
    for turn_index in range(ITERS):
        cube = current.reshape(layers_deep, edge_cells, edge_cells, edge_cells, fields)
        top_face = cube[0, :, :, 0, :].reshape(face_nodes, fields)
        gathered = lax.all_gather(top_face, "surf", axis=0, tiled=True)
        ordered = jnp.take(gathered, group_map, axis=0)
        partial_value = jnp.dot(
            operator_rows, ordered, precision=highest, preferred_element_type=jnp.float32
        )
        summed = lax.psum_scatter(
            partial_value.reshape(face_nodes, -1, fields), "col", scatter_dimension=1, tiled=True
        )
        traction_rows = summed.reshape(face_nodes, fields)
        outgoing_back = (
            jnp.zeros((surf_count * per_pair, fields), jnp.float32)
            .at[slot_index]
            .set(traction_rows)
        )
        returned = lax.all_to_all(
            outgoing_back.reshape(surf_count, per_pair, fields),
            "surf",
            split_axis=0,
            concat_axis=0,
            tiled=True,
        )
        on_top = jnp.take(returned.reshape(surf_count * per_pair, fields), send_index, axis=0)
        applied = volume_apply(current, kmats, edge_cells, layers_deep, fields)
        applied = applied.at[0, :, :, 0, :].add(on_top.reshape(edge_cells, edge_cells, fields))
        residual = load_cube - applied
        current = (cube + damping * residual).reshape(layers_deep, node_count, fields)
    return (current[None], traction_rows[None])


def solution(mesh):
    in_specs = (
        P(("surf", "col"), None, None, None),
        P(("surf", "col"), None, None, None),
        P(("surf", "col"), None, None, None),
        P("surf", None, "col"),
        P("col", None),
    )
    out_specs = (P(("surf", "col"), None, None, None), P("col", "surf", None))
    return jax.shard_map(shards, mesh=mesh, in_specs=in_specs, out_specs=out_specs, check_vma=False)
```

profile of v0, /device:TPU:1, one launch (start us, length us, event | category | flops | bytes accessed | tf_op | source)
XLA Modules:
  0.0 254.0 jit_solution(10524862129218521562)
XLA Ops:
  11.2 4.6 %collective-permute-start = (f32[3,1,8,8,256]{4,2,1,0,3:T(8,128)}, f32[3,1,8,8,256]{4,2,1,0,3:T(8,128)}, u32[]{:S(2)}, u32[]{:S(2)}) collective-permute-start(f32[3,1,8,8,256]{4,2,1,0,3:T(8,128)} %slice.588), channel_id=1, source_target_pairs={{0,4},{4,8},{8,12},{12,16},{16,20},{20,24},{24,28},{1,5},{5,9},{9,... | collective-permute-start | bytes 589832 | tf_op jit(solution)/shard_map/ppermute | solution.py:17
  16.9 28.2 %all_gather.6 = f32[512,256]{1,0:T(8,128)} all-gather(f32[64,256]{1,0:T(8,128)S(1)} %bitcast.136), channel_id=1, replica_groups=mesh['surf'=8,'col'=4] {'surf'}, dimensions={0}, use_global_device_ids=true | all-gather | bytes 589824 | tf_op jit(solution)/shard_map/all_gather | solution.py:78
  54.9 5.4 %fusion.2 = f32[3,512,256]{2,1,0:T(8,128)} fusion(f32[1,3,512,512]{3,2,1,0:T(8,128)S(1)} %copy-done, f32[1,3,512,256]{3,2,1,0:T(8,128)} %param.39), kind=kOutput, calls=%fused_computation.8 | convolution fusion | flops 2415919104 | bytes 6291456 | tf_op jit(solution)/shard_map/dab,dbf->daf/dot_general | solution.py:39
  60.4 3.8 %sort.17 = (s32[512]{0:T(512)}, s32[512]{0:T(512)S(1)}) sort(s32[512]{0:T(512)S(1)} %bitcast.141, s32[512]{0:T(512)S(1)} %iota.11), dimensions={0}, to_apply=%region_3.5 | sort | flops 4608 | bytes 8192 | tf_op jit(solution)/shard_map/jit(argsort)/sort | solution.py:61
  68.8 3.3 %collective-permute-done.1 = f32[3,1,8,8,256]{4,2,1,0,3:T(8,128)S(1)} collective-permute-done((f32[3,1,8,8,256]{4,2,1,0,3:T(8,128)S(1)}, f32[3,1,8,8,256]{4,2,1,0,3:T(8,128)S(1)}, u32[]{:S(2)}, u32[]{:S(2)}) %collective-permute-start.1) | collective-permute-done | bytes 196640 | tf_op jit(solution)/shard_map/ppermute | solution.py:20
  74.9 10.4 %collective-permute-start.2 = (f32[3,10,1,8,256]{4,2,1,0,3:T(1,128)}, f32[3,10,1,8,256]{4,2,1,0,3:T(1,128)}, u32[]{:S(2)}, u32[]{:S(2)}) collective-permute-start(f32[3,10,1,8,256]{4,2,1,0,3:T(1,128)} %get-tuple-element.181), channel_id=1, source_target_pairs={{0,1},{1,2},{2,3},{4,5},{5,6},{6,7},{8,9},{9,10},{10,11},{12,13},{... | collective-permute-start | bytes 737288 | tf_op jit(solution)/shard_map/ppermute | solution.py:17
  89.1 3.4 %all-to-all-start = ((f32[8,8,256]{2,1,0:T(8,128)}), f32[8,8,256]{2,1,0:T(8,128)S(1)}, u32[]{:S(2)}, u32[]{:S(2)}) async-start(f32[8,8,256]{2,1,0:T(8,128)} %bitcast.16), calls=%async_computation.1 | async-start | bytes 131072 | tf_op jit(solution)/shard_map/all_to_all | solution.py:92
  95.0 4.5 %scatter-add.50 = f32[3,8,8,8,256]{4,2,1,0,3:T(8,128)} dynamic-update-slice(f32[3,8,8,8,256]{4,2,1,0,3:T(8,128)} %get-tuple-element.193, f32[3,8,1,8,256]{4,2,1,0,3:T(1,128)S(1)} %fusion.25, s32[]{:T(128)} %constant.397.clone.1, s32[]{:T(128)} %constant.397.clone.1, s32[]{:T(128)} %constant.397.clone.1, s32[]{:T(128)} %constant.397.clone.1, s32[]{:T(128)} %constant.397.clone.1) | dynamic-update-slice | bytes 393220 | tf_op jit(solution)/shard_map/scatter-add | solution.py:32
  101.9 4.5 %scatter-add.51 = f32[3,8,8,8,256]{4,2,1,0,3:T(8,128)} dynamic-update-slice(f32[3,8,8,8,256]{4,2,1,0,3:T(8,128)} %scatter-add.50, f32[3,8,1,8,256]{4,2,1,0,3:T(1,128)S(1)} %fusion.24, s32[]{:T(128)} %constant.397.clone.1, s32[]{:T(128)} %constant.397.clone.1, s32[]{:T(128)} %constant.398.clone.1, s32[]{:T(128)} %constant.397.clone.1, s32[]{:T(128)} %constant.397.clone.1) | dynamic-update-slice | bytes 393220 | tf_op jit(solution)/shard_map/scatter-add | solution.py:33
  108.1 3.5 %copy.78 = f32[3,8,8,8,256]{4,3,2,1,0:T(8,128)} copy(f32[3,8,8,8,256]{4,2,1,0,3:T(8,128)} %fusion.23) | data formatting | bytes 3145728 | tf_op jit(solution)/shard_map/scatter-add | solution.py:37
  114.3 4.0 %scatter-add.55 = f32[3,8,8,8,256]{4,3,2,1,0:T(8,128)} dynamic-update-slice(f32[3,8,8,8,256]{4,3,2,1,0:T(8,128)} %copy.78, f32[2,8,8,1,256]{4,3,2,1,0:T(1,128)S(1)} %fusion.27, s32[]{:T(128)} %constant.399.clone.1, s32[]{:T(128)} %constant.397.clone.1, s32[]{:T(128)} %constant.397.clone.1, s32[]{:T(128)} %constant.397.clone.1, s32[]{:T(128)} %constant.397.clone.1) | dynamic-update-slice | bytes 262148 | tf_op jit(solution)/shard_map/scatter-add | solution.py:38
  118.3 3.3 %multiply_add_fusion.3 = f32[3,8,8,8,256]{4,3,2,1,0:T(8,128)} fusion(f32[3,8,8,8,256]{4,3,2,1,0:T(8,128)} %bitcast.130, f32[3,8,8,8,256]{4,3,2,1,0:T(8,128)} %scatter-add.55), kind=kLoop, calls=%fused_computation.14 | loop fusion | flops 786432 | bytes 4718592 | tf_op jit(solution)/shard_map/add | solution.py:40
  131.6 3.7 %collective-permute-start.4 = (f32[3,1,8,8,256]{4,2,1,0,3:T(8,128)}, f32[3,1,8,8,256]{4,2,1,0,3:T(8,128)}, u32[]{:S(2)}, u32[]{:S(2)}) collective-permute-start(f32[3,1,8,8,256]{4,2,1,0,3:T(8,128)} %slice.605), channel_id=1, source_target_pairs={{0,4},{4,8},{8,12},{12,16},{16,20},{20,24},{24,28},{1,5},{5,9},{9,... | collective-permute-start | bytes 589832 | tf_op jit(solution)/shard_map/ppermute | solution.py:17
  135.3 28.4 %all_gather.7 = f32[512,256]{1,0:T(8,128)} all-gather(f32[64,256]{1,0:T(8,128)S(1)} %bitcast.137), channel_id=1, replica_groups=mesh['surf'=8,'col'=4] {'surf'}, dimensions={0}, use_global_device_ids=true | all-gather | bytes 589824 | tf_op jit(solution)/shard_map/all_gather | solution.py:78
  163.7 3.3 %gather_fusion.2 = f32[512,256]{1,0:T(8,128)} fusion(f32[512,256]{1,0:T(8,128)} %all_gather.7, s32[1024]{0:T(1024)S(1)} %pad_clamp_fusion.1), kind=kCustom, calls=%fused_computation.2.clone | custom fusion | bytes 1050624 | tf_op jit(solution)/shard_map/jit(_take)/gather | solution.py:79
  175.8 4.6 %collective-permute-done.5 = f32[3,1,8,8,256]{4,2,1,0,3:T(8,128)S(1)} collective-permute-done((f32[3,1,8,8,256]{4,2,1,0,3:T(8,128)S(1)}, f32[3,1,8,8,256]{4,2,1,0,3:T(8,128)S(1)}, u32[]{:S(2)}, u32[]{:S(2)}) %collective-permute-start.5) | collective-permute-done | bytes 196640 | tf_op jit(solution)/shard_map/ppermute | solution.py:20
  183.2 10.5 %collective-permute-start.6 = (f32[3,10,1,8,256]{4,2,1,0,3:T(1,128)}, f32[3,10,1,8,256]{4,2,1,0,3:T(1,128)}, u32[]{:S(2)}, u32[]{:S(2)}) collective-permute-start(f32[3,10,1,8,256]{4,2,1,0,3:T(1,128)} %get-tuple-element.179), channel_id=1, source_target_pairs={{0,1},{1,2},{2,3},{4,5},{5,6},{6,7},{8,9},{9,10},{10,11},{12,13},{... | collective-permute-start | bytes 737288 | tf_op jit(solution)/shard_map/ppermute | solution.py:17
  193.7 6.5 %fusion.5 = f32[3,512,256]{1,2,0:T(8,128)} fusion(f32[3,512,256]{2,1,0:T(8,128)S(1)} %bitcast.120, f32[1,3,512,512]{3,2,1,0:T(8,128)S(1)} %copy-done), kind=kOutput, calls=%fused_computation.15 | convolution fusion | flops 2415919104 | bytes 6291456 | tf_op jit(solution)/shard_map/dab,dbf->daf/dot_general | solution.py:39
  208.8 3.3 %all-to-all-start.1 = ((f32[8,8,256]{2,1,0:T(8,128)}), f32[8,8,256]{2,1,0:T(8,128)S(1)}, u32[]{:S(2)}, u32[]{:S(2)}) async-start(f32[8,8,256]{2,1,0:T(8,128)} %bitcast.26), calls=%async_computation.3 | async-start | bytes 131072 | tf_op jit(solution)/shard_map/all_to_all | solution.py:92
  214.0 4.5 %scatter-add.61 = f32[3,8,8,8,256]{4,2,1,0,3:T(8,128)} dynamic-update-slice(f32[3,8,8,8,256]{4,2,1,0,3:T(8,128)} %get-tuple-element.191, f32[3,8,1,8,256]{4,2,1,0,3:T(1,128)S(1)} %fusion.19, s32[]{:T(128)} %constant.397.clone.1, s32[]{:T(128)} %constant.397.clone.1, s32[]{:T(128)} %constant.397.clone.1, s32[]{:T(128)} %constant.397.clone.1, s32[]{:T(128)} %constant.397.clone.1) | dynamic-update-slice | bytes 393220 | tf_op jit(solution)/shard_map/scatter-add | solution.py:32
  220.4 4.5 %scatter-add.64 = f32[3,8,8,8,256]{4,2,1,0,3:T(8,128)} dynamic-update-slice(f32[3,8,8,8,256]{4,2,1,0,3:T(8,128)} %scatter-add.61, f32[3,8,1,8,256]{4,2,1,0,3:T(1,128)S(1)} %fusion.18, s32[]{:T(128)} %constant.397.clone.1, s32[]{:T(128)} %constant.397.clone.1, s32[]{:T(128)} %constant.398.clone.1, s32[]{:T(128)} %constant.397.clone.1, s32[]{:T(128)} %constant.397.clone.1) | dynamic-update-slice | bytes 393220 | tf_op jit(solution)/shard_map/scatter-add | solution.py:33
  229.3 3.5 %copy.90 = f32[3,8,8,8,256]{4,3,2,1,0:T(8,128)} copy(f32[3,8,8,8,256]{4,2,1,0,3:T(8,128)} %fusion.17) | data formatting | bytes 3145728 | tf_op jit(solution)/shard_map/scatter-add | solution.py:37
  233.5 4.0 %scatter-add.66 = f32[3,8,8,8,256]{4,3,2,1,0:T(8,128)} dynamic-update-slice(f32[3,8,8,8,256]{4,3,2,1,0:T(8,128)} %copy.90, f32[2,8,8,1,256]{4,3,2,1,0:T(1,128)S(1)} %fusion.26, s32[]{:T(128)} %constant.399.clone.1, s32[]{:T(128)} %constant.397.clone.1, s32[]{:T(128)} %constant.397.clone.1, s32[]{:T(128)} %constant.397.clone.1, s32[]{:T(128)} %constant.397.clone.1) | dynamic-update-slice | bytes 262148 | tf_op jit(solution)/shard_map/scatter-add | solution.py:38
  243.2 3.9 %multiply_add_fusion = f32[3,8,8,8,256]{4,3,2,1,0:T(8,128)} fusion(f32[3,8,8,8,256]{4,3,2,1,0:T(8,128)} %copy-done.1, f32[3,8,8,8,256]{4,3,2,1,0:T(8,128)} %bitcast.129, f32[3,8,8,8,256]{4,3,2,1,0:T(8,128)} %scatter-add.69), kind=kLoop, calls=%fused_computation.11 | loop fusion | flops 1179648 | bytes 6291456 | tf_op jit(solution)/shard_map/add | solution.py:103
  (102 shorter events, 79.9 us)
Async XLA Ops:
  7.2 47.8 %copy-start = (f32[1,3,512,512]{3,2,1,0:T(8,128)S(1)}, f32[1,3,512,512]{3,2,1,0:T(8,128)}, u32[]{:S(2)}) copy-start(f32[1,3,512,512]{3,2,1,0:T(8,128)} %param.37) | copy-start | bytes 9437188
  7.2 80.2 %reduce-scatter.3.cloned.1.call-start = ((), (), s32[]{:S(2)}) async-start(), calls=%async_computation.4 | async-start | bytes 327680 | tf_op jit(solution)/shard_map/reduce_scatter | solution.py:83
  7.2 9.6 %copy-start.7 = (s32[1,512]{1,0:T(1,128)S(1)}, s32[1,512]{1,0:T(1,128)}, u32[]{:S(2)}) copy-start(s32[1,512]{1,0:T(1,128)} %param.41) | copy-start | bytes 6148
  9.3 1.2 copy-start.5
  11.2 53.5 %collective-permute-start = (f32[3,1,8,8,256]{4,2,1,0,3:T(8,128)}, f32[3,1,8,8,256]{4,2,1,0,3:T(8,128)}, u32[]{:S(2)}, u32[]{:S(2)}) collective-permute-start(f32[3,1,8,8,256]{4,2,1,0,3:T(8,128)} %slice.588), channel_id=1, source_target_pairs={{0,4},{4,8},{8,12},{12,16},{16,20},{20,24},{24,28},{1,5},{5,9},{9,... | collective-permute-start | bytes 589832 | tf_op jit(solution)/shard_map/ppermute | solution.py:17
  64.2 4.2 %copy-start.3 = (f32[1,3,512,256]{3,2,1,0:T(8,128)S(1)}, f32[1,3,512,256]{3,2,1,0:T(8,128)}, u32[]{:S(2)}) copy-start(f32[1,3,512,256]{3,2,1,0:T(8,128)} %param.39) | copy-start | bytes 4718596
  65.8 6.4 %collective-permute-start.1 = (f32[3,1,8,8,256]{4,2,1,0,3:T(8,128)S(1)}, f32[3,1,8,8,256]{4,2,1,0,3:T(8,128)S(1)}, u32[]{:S(2)}, u32[]{:S(2)}) collective-permute-start(f32[3,1,8,8,256]{4,2,1,0,3:T(8,128)S(1)} %get-tuple-element.186), channel_id=1, source_target_pairs={{4,0},{8,4},{12,8},{16,12},{20,16},{24,20},{28,24},{5,1},{9,5},{13... | collective-permute-start | bytes 589832 | tf_op jit(solution)/shard_map/ppermute | solution.py:20
  74.9 17.8 %collective-permute-start.2 = (f32[3,10,1,8,256]{4,2,1,0,3:T(1,128)}, f32[3,10,1,8,256]{4,2,1,0,3:T(1,128)}, u32[]{:S(2)}, u32[]{:S(2)}) collective-permute-start(f32[3,10,1,8,256]{4,2,1,0,3:T(1,128)} %get-tuple-element.181), channel_id=1, source_target_pairs={{0,1},{1,2},{2,3},{4,5},{5,6},{6,7},{8,9},{9,10},{10,11},{12,13},{... | collective-permute-start | bytes 737288 | tf_op jit(solution)/shard_map/ppermute | solution.py:17
  85.5 3.7 %copy-start.8 = (s32[64]{0:T(128)}, s32[64]{0:T(128)S(1)}, u32[]{:S(2)}) copy-start(s32[64]{0:T(128)S(1)} %fusion.36) | copy-start | bytes 772
  85.5 14.0 %collective-permute-start.3 = (f32[3,10,1,8,256]{4,2,1,0,3:T(1,128)}, f32[3,10,1,8,256]{4,2,1,0,3:T(1,128)}, u32[]{:S(2)}, u32[]{:S(2)}) collective-permute-start(f32[3,10,1,8,256]{4,2,1,0,3:T(1,128)} %get-tuple-element.180), channel_id=1, source_target_pairs={{1,0},{2,1},{3,2},{5,4},{6,5},{7,6},{9,8},{10,9},{11,10},{13,12},{... | collective-permute-start | bytes 737288 | tf_op jit(solution)/shard_map/ppermute | solution.py:20
  89.1 32.5 %all-to-all-start = ((f32[8,8,256]{2,1,0:T(8,128)}), f32[8,8,256]{2,1,0:T(8,128)S(1)}, u32[]{:S(2)}, u32[]{:S(2)}) async-start(f32[8,8,256]{2,1,0:T(8,128)} %bitcast.16), calls=%async_computation.1 | async-start | bytes 131072 | tf_op jit(solution)/shard_map/all_to_all | solution.py:92
  92.5 114.6 %reduce-scatter.5.cloned.1.call-start = ((), (), s32[]{:S(2)}) async-start(), calls=%async_computation.5 | async-start | bytes 327680 | tf_op jit(solution)/shard_map/reduce_scatter | solution.py:83
  128.6 1.1 copy-start.1
  129.7 1.2 copy-start.6
  131.6 39.9 %collective-permute-start.4 = (f32[3,1,8,8,256]{4,2,1,0,3:T(8,128)}, f32[3,1,8,8,256]{4,2,1,0,3:T(8,128)}, u32[]{:S(2)}, u32[]{:S(2)}) collective-permute-start(f32[3,1,8,8,256]{4,2,1,0,3:T(8,128)} %slice.605), channel_id=1, source_target_pairs={{0,4},{4,8},{8,12},{12,16},{16,20},{20,24},{24,28},{1,5},{5,9},{9,... | collective-permute-start | bytes 589832 | tf_op jit(solution)/shard_map/ppermute | solution.py:17
  171.4 3.9 %copy-start.2 = (f32[3,8,8,8,256]{4,3,2,1,0:T(8,128)S(1)}, f32[3,8,8,8,256]{4,3,2,1,0:T(8,128)}, u32[]{:S(2)}) copy-start(f32[3,8,8,8,256]{4,3,2,1,0:T(8,128)} %copy-done.1) | copy-start | bytes 4718596
  174.0 6.4 %collective-permute-start.5 = (f32[3,1,8,8,256]{4,2,1,0,3:T(8,128)S(1)}, f32[3,1,8,8,256]{4,2,1,0,3:T(8,128)S(1)}, u32[]{:S(2)}, u32[]{:S(2)}) collective-permute-start(f32[3,1,8,8,256]{4,2,1,0,3:T(8,128)S(1)} %get-tuple-element.184), channel_id=1, source_target_pairs={{4,0},{8,4},{12,8},{16,12},{20,16},{24,20},{28,24},{5,1},{9,5},{13... | collective-permute-start | bytes 589832 | tf_op jit(solution)/shard_map/ppermute | solution.py:20
  183.2 28.9 %collective-permute-start.6 = (f32[3,10,1,8,256]{4,2,1,0,3:T(1,128)}, f32[3,10,1,8,256]{4,2,1,0,3:T(1,128)}, u32[]{:S(2)}, u32[]{:S(2)}) collective-permute-start(f32[3,10,1,8,256]{4,2,1,0,3:T(1,128)} %get-tuple-element.179), channel_id=1, source_target_pairs={{0,1},{1,2},{2,3},{4,5},{5,6},{6,7},{8,9},{9,10},{10,11},{12,13},{... | collective-permute-start | bytes 737288 | tf_op jit(solution)/shard_map/ppermute | solution.py:17
  205.1 13.3 %collective-permute-start.7 = (f32[3,10,1,8,256]{4,2,1,0,3:T(1,128)}, f32[3,10,1,8,256]{4,2,1,0,3:T(1,128)}, u32[]{:S(2)}, u32[]{:S(2)}) collective-permute-start(f32[3,10,1,8,256]{4,2,1,0,3:T(1,128)} %get-tuple-element.178), channel_id=1, source_target_pairs={{1,0},{2,1},{3,2},{5,4},{6,5},{7,6},{9,8},{10,9},{11,10},{13,12},{... | collective-permute-start | bytes 737288 | tf_op jit(solution)/shard_map/ppermute | solution.py:20
  208.8 24.0 %all-to-all-start.1 = ((f32[8,8,256]{2,1,0:T(8,128)}), f32[8,8,256]{2,1,0:T(8,128)S(1)}, u32[]{:S(2)}, u32[]{:S(2)}) async-start(f32[8,8,256]{2,1,0:T(8,128)} %bitcast.26), calls=%async_computation.3 | async-start | bytes 131072 | tf_op jit(solution)/shard_map/all_to_all | solution.py:92
  239.6 1.2 copy-start.4
Sparse Core Ops, SparseCore 0:
  55.0 24.3 reduce-scatter.2
  171.5 24.3 reduce-scatter.4
where the time goes:
time: 256 us; the launch traced here: 254 us
  local copies, waits for them, and re-layouts  77.7 us (30%)
  blocking collectives  56.6 us (22%)
  starting transfers between devices  42.6 us (17%)
  other arithmetic  38.9 us (15%)
  matrix products  15.7 us (6%)
  between operations  14.4 us (6%)
  waiting for transfers between devices  8.06 us (3%)
    all_gather x2, blocking collectives, shards(): gathered = lax.all_gather(top_face, 'surf', axis=0, tiled=True)  56.6 us
    ppermute x4, starting transfers between devices, with_halo(): lax.ppermute(lax.slice_in_dim(block, block.shape[dim] - width, None, axis...  29.2 us
    dot_general x2, matrix products, volume_apply(): applied = jnp.einsum('dab,dbf->daf', kmats, current, precision=highest)  11.9 us
    scatter-add x2, local copies, waits for them, and re-layouts, volume_apply(): extra = extra.at[:, :, 0].add(cube[:, :, 0] - padded[:, 1:-1, 0])  8.99 us
    scatter-add x2, local copies, waits for them, and re-layouts, volume_apply(): extra = extra.at[:, :, -1].add(cube[:, :, -1] - padded[:, 1:-1, -1])  8.99 us
    scatter-add x2, local copies, waits for them, and re-layouts, volume_apply(): extra = extra.at[1:, :, :, 0].add(low_k[1:] - high_k[:-1])  8 us
    ppermute x4, waiting for transfers between devices, with_halo(): lax.ppermute(lax.slice_in_dim(block, 0, width, axis=dim), axis, backward)  7.97 us
    scatter-add x2, local copies, waits for them, and re-layouts, volume_apply(): extra = extra.at[:, :, :, -1].add(high_k - deeper)  6.98 us
  transfers between devices with their start and end apart: 12, of which 2 were waited for; matrix products, arithmetic and copies ran while one was open for 41% of the time, Pallas kernels for 0%

commit v1 on v0

--- a/solution.py
+++ b/solution.py
@@ -75,7 +75,25 @@
     for turn_index in range(ITERS):
         cube = current.reshape(layers_deep, edge_cells, edge_cells, edge_cells, fields)
         top_face = cube[0, :, :, 0, :].reshape(face_nodes, fields)
-        gathered = lax.all_gather(top_face, "surf", axis=0, tiled=True)
+        size, position, width_2 = (lax.axis_size("surf"), lax.axis_index("surf"), top_face.shape[0])
+        right = [(i_2, (i_2 + 1) % size) for i_2 in range(size)]
+        left = [(i_2, (i_2 - 1) % size) for i_2 in range(size)]
+        gathered = jnp.zeros(
+            (*top_face.shape[:0], size * width_2, *top_face.shape[0 + 1 :]), top_face.dtype
+        )
+        gathered = lax.dynamic_update_slice_in_dim(gathered, top_face, position * width_2, axis=0)
+        from_left = from_right = top_face
+        half = size // 2
+        for step in range(1, half + 1):
+            from_left = lax.ppermute(from_left, "surf", right)
+            gathered = lax.dynamic_update_slice_in_dim(
+                gathered, from_left, (position - step) % size * width_2, axis=0
+            )
+            if step < size - half:
+                from_right = lax.ppermute(from_right, "surf", left)
+                gathered = lax.dynamic_update_slice_in_dim(
+                    gathered, from_right, (position + step) % size * width_2, axis=0
+                )
         ordered = jnp.take(gathered, group_map, axis=0)
         partial_value = jnp.dot(
             operator_rows, ordered, precision=highest, preferred_element_type=jnp.float32

time: 256 us -> 241 us (0.941)
  blocking collectives: 56.6 us -> 0 us
  local copies, waits for them, and re-layouts: 77.7 us -> 98.3 us
  starting transfers between devices: 42.6 us -> 61.7 us
  other arithmetic: 38.9 us -> 43.2 us
    all_gather x2 -> x0, blocking collectives: 56.6 us -> none  [shards(): gathered = lax.all_gather(top_face, 'surf', axis=0, tiled=True)]
    ppermute x0 -> x14, starting transfers between devices: none -> 28.3 us  [the longest x6 23.5 us: shards(): from_right = lax.ppermute(from_right, 'surf', left)]
    dynamic_update_slice x0 -> x16, local copies, waits for them, and re-layouts: none -> 12.7 us  [the longest x8 6.74 us: shards(): lax.dynamic_update_slice_in_dim(gathered, from_left, (position - step) %...]
    ppermute x4, starting transfers between devices: 29.2 us -> 18.1 us  [with_halo(): lax.ppermute(lax.slice_in_dim(block, block.shape[dim] - width, None, axis...]
    ppermute x4, waiting for transfers between devices: 7.97 us -> 0.01 us  [with_halo(): lax.ppermute(lax.slice_in_dim(block, 0, width, axis=dim), axis, backward)]
    all_to_all x2, waiting for transfers between devices: 0.01 us -> 4.76 us  [shards(): lax.all_to_all(outgoing_back.reshape(surf_count, per_pair, fields), 'surf...]
    slice x2, local copies, waits for them, and re-layouts: 2.19 us -> 6.6 us  [with_halo(): lax.slice_in_dim(block, 0, width, axis=dim)]
    ppermute x0 -> x14, waiting for transfers between devices: none -> 3.23 us  [the longest x8 3.08 us: shards(): from_left = lax.ppermute(from_left, 'surf', right)]
  transfers between devices with their start and end apart: 12 -> 26, of which waited for: 2 -> 5; matrix products, arithmetic and copies ran while one was open for 41% -> 51% of each run, Pallas kernels for 0% -> 0%
where the time goes in v1:
time: 241 us; the launch traced here: 239 us
  local copies, waits for them, and re-layouts  98.3 us (41%)
  starting transfers between devices  61.7 us (26%)
  other arithmetic  43.2 us (18%)
  between operations  14.6 us (6%)
  matrix products  13.4 us (6%)
  waiting for transfers between devices  8.04 us (3%)
    ppermute x6, starting transfers between devices, shards(): from_right = lax.ppermute(from_right, 'surf', left)  23.5 us
    ppermute x4, starting transfers between devices, with_halo(): lax.ppermute(lax.slice_in_dim(block, block.shape[dim] - width, None, axis...  18.1 us
    dot_general x2, matrix products, volume_apply(): applied = jnp.einsum('dab,dbf->daf', kmats, current, precision=highest)  11.9 us
    scatter-add x2, local copies, waits for them, and re-layouts, volume_apply(): extra = extra.at[:, :, 0].add(cube[:, :, 0] - padded[:, 1:-1, 0])  9.02 us
    scatter-add x2, local copies, waits for them, and re-layouts, volume_apply(): extra = extra.at[:, :, -1].add(cube[:, :, -1] - padded[:, 1:-1, -1])  9 us
    all_to_all x2, starting transfers between devices, shards(): lax.all_to_all(outgoing_back.reshape(surf_count, per_pair, fields), 'surf...  8.64 us
    scatter-add x2, local copies, waits for them, and re-layouts, volume_apply(): extra = extra.at[1:, :, :, 0].add(low_k[1:] - high_k[:-1])  8.01 us
    scatter-add x2, local copies, waits for them, and re-layouts, volume_apply(): extra = extra.at[:, :, :, -1].add(high_k - deeper)  7.02 us
  transfers between devices with their start and end apart: 26, of which 5 were waited for; matrix products, arithmetic and copies ran while one was open for 51% of the time, Pallas kernels for 0%

profile of v1, /device:TPU:1, one launch (start us, length us, event | category | flops | bytes accessed | tf_op | source)
XLA Modules:
  0.0 239.2 jit_solution(15915059950088302391)
XLA Ops:
  21.4 5.4 %fusion.2 = f32[3,512,256]{2,1,0:T(8,128)} fusion(f32[1,3,512,512]{3,2,1,0:T(8,128)S(1)} %copy-done, f32[1,3,512,256]{3,2,1,0:T(8,128)} %param.39), kind=kOutput, calls=%fused_computation.8 | convolution fusion | flops 2415919104 | bytes 6291456 | tf_op jit(solution)/shard_map/dab,dbf->daf/dot_general | solution.py:39
  30.4 3.8 %sort.17 = (s32[512]{0:T(512)}, s32[512]{0:T(512)S(1)}) sort(s32[512]{0:T(512)S(1)} %bitcast.143, s32[512]{0:T(512)S(1)} %iota.11), dimensions={0}, to_apply=%region_3.5 | sort | flops 4608 | bytes 8192 | tf_op jit(solution)/shard_map/jit(argsort)/sort | solution.py:61
  35.8 3.6 %collective-permute-start.7 = (f32[64,256]{1,0:T(8,128)S(1)}, f32[64,256]{1,0:T(8,128)S(1)}, u32[]{:S(2)}, u32[]{:S(2)}) collective-permute-start(f32[64,256]{1,0:T(8,128)S(1)} %collective-permute-done.5), channel_id=1, source_target_pairs={{0,28},{4,0},{8,4},{12,8},{16,12},{20,16},{24,20},{28,24},{1,29},{... | collective-permute-start | bytes 196616 | tf_op jit(solution)/shard_map/ppermute | solution.py:93
  41.6 4.2 %collective-permute-start.9 = (f32[64,256]{1,0:T(8,128)S(1)}, f32[64,256]{1,0:T(8,128)S(1)}, u32[]{:S(2)}, u32[]{:S(2)}) collective-permute-start(f32[64,256]{1,0:T(8,128)S(1)} %collective-permute-done.7), channel_id=1, source_target_pairs={{0,28},{4,0},{8,4},{12,8},{16,12},{20,16},{24,20},{28,24},{1,29},{... | collective-permute-start | bytes 196616 | tf_op jit(solution)/shard_map/ppermute | solution.py:93
  63.1 6.5 %collective-permute-start.2 = (f32[3,10,1,8,256]{4,2,1,0,3:T(1,128)}, f32[3,10,1,8,256]{4,2,1,0,3:T(1,128)}, u32[]{:S(2)}, u32[]{:S(2)}) collective-permute-start(f32[3,10,1,8,256]{4,2,1,0,3:T(1,128)} %get-tuple-element.181), channel_id=1, source_target_pairs={{0,1},{1,2},{2,3},{4,5},{5,6},{6,7},{8,9},{9,10},{10,11},{12,13},{... | collective-permute-start | bytes 737288 | tf_op jit(solution)/shard_map/ppermute | solution.py:17
  77.3 4.5 %scatter-add.50 = f32[3,8,8,8,256]{4,2,1,0,3:T(8,128)} dynamic-update-slice(f32[3,8,8,8,256]{4,2,1,0,3:T(8,128)} %get-tuple-element.193, f32[3,8,1,8,256]{4,2,1,0,3:T(1,128)S(1)} %fusion.25, s32[]{:T(128)} %constant.454.clone.1, s32[]{:T(128)} %constant.454.clone.1, s32[]{:T(128)} %constant.454.clone.1, s32[]{:T(128)} %constant.454.clone.1, s32[]{:T(128)} %constant.454.clone.1) | dynamic-update-slice | bytes 393220 | tf_op jit(solution)/shard_map/scatter-add | solution.py:32
  84.2 4.5 %scatter-add.51 = f32[3,8,8,8,256]{4,2,1,0,3:T(8,128)} dynamic-update-slice(f32[3,8,8,8,256]{4,2,1,0,3:T(8,128)} %scatter-add.50, f32[3,8,1,8,256]{4,2,1,0,3:T(1,128)S(1)} %fusion.24, s32[]{:T(128)} %constant.454.clone.1, s32[]{:T(128)} %constant.454.clone.1, s32[]{:T(128)} %constant.455.clone.1, s32[]{:T(128)} %constant.454.clone.1, s32[]{:T(128)} %constant.454.clone.1) | dynamic-update-slice | bytes 393220 | tf_op jit(solution)/shard_map/scatter-add | solution.py:33
  90.5 3.5 %copy.78 = f32[3,8,8,8,256]{4,3,2,1,0:T(8,128)} copy(f32[3,8,8,8,256]{4,2,1,0,3:T(8,128)} %fusion.23) | data formatting | bytes 3145728 | tf_op jit(solution)/shard_map/scatter-add | solution.py:37
  96.7 4.0 %scatter-add.55 = f32[3,8,8,8,256]{4,3,2,1,0:T(8,128)} dynamic-update-slice(f32[3,8,8,8,256]{4,3,2,1,0:T(8,128)} %copy.78, f32[2,8,8,1,256]{4,3,2,1,0:T(1,128)S(1)} %fusion.27, s32[]{:T(128)} %constant.456.clone.1, s32[]{:T(128)} %constant.454.clone.1, s32[]{:T(128)} %constant.454.clone.1, s32[]{:T(128)} %constant.454.clone.1, s32[]{:T(128)} %constant.454.clone.1) | dynamic-update-slice | bytes 262148 | tf_op jit(solution)/shard_map/scatter-add | solution.py:38
  102.4 5.3 %all-to-all-start = ((f32[8,8,256]{2,1,0:T(8,128)}), f32[8,8,256]{2,1,0:T(8,128)S(1)}, u32[]{:S(2)}, u32[]{:S(2)}) async-start(f32[8,8,256]{2,1,0:T(8,128)} %bitcast.16), calls=%async_computation.1 | async-start | bytes 131072 | tf_op jit(solution)/shard_map/all_to_all | solution.py:110
  107.7 3.3 %multiply_add_fusion.3 = f32[3,8,8,8,256]{4,3,2,1,0:T(8,128)} fusion(f32[3,8,8,8,256]{4,3,2,1,0:T(8,128)} %bitcast.134, f32[3,8,8,8,256]{4,3,2,1,0:T(8,128)} %scatter-add.55), kind=kLoop, calls=%fused_computation.14 | loop fusion | flops 786432 | bytes 4718592 | tf_op jit(solution)/shard_map/add | solution.py:40
  121.3 4.1 %collective-permute-start.16 = (f32[64,256]{1,0:T(8,128)}, f32[64,256]{1,0:T(8,128)}, u32[]{:S(2)}, u32[]{:S(2)}) collective-permute-start(f32[64,256]{1,0:T(8,128)} %bitcast.122), channel_id=1, source_target_pairs={{0,28},{4,0},{8,4},{12,8},{16,12},{20,16},{24,20},{28,24},{1,29},{... | collective-permute-start | bytes 196616 | tf_op jit(solution)/shard_map/ppermute | solution.py:93
  126.2 6.5 %fusion.5 = f32[3,512,256]{1,2,0:T(8,128)} fusion(f32[3,512,256]{2,1,0:T(8,128)S(1)} %bitcast.124, f32[1,3,512,512]{3,2,1,0:T(8,128)S(1)} %copy-done), kind=kOutput, calls=%fused_computation.15 | convolution fusion | flops 2415919104 | bytes 6291456 | tf_op jit(solution)/shard_map/dab,dbf->daf/dot_general | solution.py:39
  142.5 4.2 %collective-permute-start.18 = (f32[64,256]{1,0:T(8,128)}, f32[64,256]{1,0:T(8,128)S(1)}, u32[]{:S(2)}, u32[]{:S(2)}) collective-permute-start(f32[64,256]{1,0:T(8,128)} %collective-permute-done.16), channel_id=1, source_target_pairs={{0,28},{4,0},{8,4},{12,8},{16,12},{20,16},{24,20},{28,24},{1,29},{... | collective-permute-start | bytes 196616 | tf_op jit(solution)/shard_map/ppermute | solution.py:93
  148.3 4.5 %collective-permute-start.20 = (f32[64,256]{1,0:T(8,128)S(1)}, f32[64,256]{1,0:T(8,128)S(1)}, u32[]{:S(2)}, u32[]{:S(2)}) collective-permute-start(f32[64,256]{1,0:T(8,128)S(1)} %collective-permute-done.18), channel_id=1, source_target_pairs={{0,28},{4,0},{8,4},{12,8},{16,12},{20,16},{24,20},{28,24},{1,29},{... | collective-permute-start | bytes 196616 | tf_op jit(solution)/shard_map/ppermute | solution.py:93
  171.9 3.3 %fusion.40 = (f32[3,10,1,8,256]{4,2,1,0,3:T(1,128)}, f32[3,10,1,8,256]{4,2,1,0,3:T(1,128)}) fusion(f32[3,10,8,8,256]{4,2,1,0,3:T(8,128)} %get-tuple-element.190), kind=kLoop, calls=%fused_computation.124 | loop fusion | bytes 983040 | tf_op jit(solution)/shard_map/slice | solution.py:20
  175.2 8.3 %collective-permute-start.13 = (f32[3,10,1,8,256]{4,2,1,0,3:T(1,128)}, f32[3,10,1,8,256]{4,2,1,0,3:T(1,128)}, u32[]{:S(2)}, u32[]{:S(2)}) collective-permute-start(f32[3,10,1,8,256]{4,2,1,0,3:T(1,128)} %get-tuple-element.179), channel_id=1, source_target_pairs={{0,1},{1,2},{2,3},{4,5},{5,6},{6,7},{8,9},{9,10},{10,11},{12,13},{... | collective-permute-start | bytes 737288 | tf_op jit(solution)/shard_map/ppermute | solution.py:17
  190.6 4.5 %scatter-add.61 = f32[3,8,8,8,256]{4,2,1,0,3:T(8,128)} dynamic-update-slice(f32[3,8,8,8,256]{4,2,1,0,3:T(8,128)} %get-tuple-element.191, f32[3,8,1,8,256]{4,2,1,0,3:T(1,128)S(1)} %fusion.19, s32[]{:T(128)} %constant.454.clone.1, s32[]{:T(128)} %constant.454.clone.1, s32[]{:T(128)} %constant.454.clone.1, s32[]{:T(128)} %constant.454.clone.1, s32[]{:T(128)} %constant.454.clone.1) | dynamic-update-slice | bytes 393220 | tf_op jit(solution)/shard_map/scatter-add | solution.py:32
  197.0 4.5 %scatter-add.64 = f32[3,8,8,8,256]{4,2,1,0,3:T(8,128)} dynamic-update-slice(f32[3,8,8,8,256]{4,2,1,0,3:T(8,128)} %scatter-add.61, f32[3,8,1,8,256]{4,2,1,0,3:T(1,128)S(1)} %fusion.18, s32[]{:T(128)} %constant.454.clone.1, s32[]{:T(128)} %constant.454.clone.1, s32[]{:T(128)} %constant.455.clone.1, s32[]{:T(128)} %constant.454.clone.1, s32[]{:T(128)} %constant.454.clone.1) | dynamic-update-slice | bytes 393220 | tf_op jit(solution)/shard_map/scatter-add | solution.py:33
  204.2 3.5 %copy.90 = f32[3,8,8,8,256]{4,3,2,1,0:T(8,128)} copy(f32[3,8,8,8,256]{4,2,1,0,3:T(8,128)} %fusion.17) | data formatting | bytes 3145728 | tf_op jit(solution)/shard_map/scatter-add | solution.py:37
  209.5 4.0 %scatter-add.66 = f32[3,8,8,8,256]{4,3,2,1,0:T(8,128)} dynamic-update-slice(f32[3,8,8,8,256]{4,3,2,1,0:T(8,128)} %copy.90, f32[2,8,8,1,256]{4,3,2,1,0:T(1,128)S(1)} %fusion.26, s32[]{:T(128)} %constant.456.clone.1, s32[]{:T(128)} %constant.454.clone.1, s32[]{:T(128)} %constant.454.clone.1, s32[]{:T(128)} %constant.454.clone.1, s32[]{:T(128)} %constant.454.clone.1) | dynamic-update-slice | bytes 262148 | tf_op jit(solution)/shard_map/scatter-add | solution.py:38
  215.2 3.3 %all-to-all-start.1 = ((f32[8,8,256]{2,1,0:T(8,128)}), f32[8,8,256]{2,1,0:T(8,128)S(1)}, u32[]{:S(2)}, u32[]{:S(2)}) async-start(f32[8,8,256]{2,1,0:T(8,128)} %bitcast.26), calls=%async_computation.3 | async-start | bytes 131072 | tf_op jit(solution)/shard_map/all_to_all | solution.py:110
  218.6 3.3 %multiply_add_fusion.1 = f32[3,8,8,8,256]{4,3,2,1,0:T(8,128)} fusion(f32[3,8,8,8,256]{4,3,2,1,0:T(8,128)} %bitcast.131, f32[3,8,8,8,256]{4,3,2,1,0:T(8,128)} %scatter-add.66), kind=kLoop, calls=%fused_computation.12 | loop fusion | flops 786432 | bytes 4718592 | tf_op jit(solution)/shard_map/add | solution.py:40
  228.5 3.9 %multiply_add_fusion = f32[3,8,8,8,256]{4,3,2,1,0:T(8,128)} fusion(f32[3,8,8,8,256]{4,3,2,1,0:T(8,128)} %copy-done.1, f32[3,8,8,8,256]{4,3,2,1,0:T(8,128)} %bitcast.133, f32[3,8,8,8,256]{4,3,2,1,0:T(8,128)} %scatter-add.69), kind=kLoop, calls=%fused_computation.11 | loop fusion | flops 1179648 | bytes 6291456 | tf_op jit(solution)/shard_map/add | solution.py:121
  (154 shorter events, 118.1 us)
Async XLA Ops:
  7.2 93.5 %reduce-scatter.3.cloned.1.call-start = ((), (), s32[]{:S(2)}) async-start(), calls=%async_computation.4 | async-start | bytes 327680 | tf_op jit(solution)/shard_map/reduce_scatter | solution.py:101
  9.1 26.1 %collective-permute-start.4 = (f32[64,256]{1,0:T(8,128)}, f32[64,256]{1,0:T(8,128)}, u32[]{:S(2)}, u32[]{:S(2)}) collective-permute-start(f32[64,256]{1,0:T(8,128)} %bitcast.123), channel_id=1, source_target_pairs={{0,4},{4,8},{8,12},{12,16},{16,20},{20,24},{24,28},{28,0},{1,5},{5... | collective-permute-start | bytes 196616 | tf_op jit(solution)/shard_map/ppermute | solution.py:88
  11.1 24.7 %collective-permute-start.5 = (f32[64,256]{1,0:T(8,128)}, f32[64,256]{1,0:T(8,128)S(1)}, u32[]{:S(2)}, u32[]{:S(2)}) collective-permute-start(f32[64,256]{1,0:T(8,128)} %bitcast.123), channel_id=1, source_target_pairs={{0,28},{4,0},{8,4},{12,8},{16,12},{20,16},{24,20},{28,24},{1,29},{... | collective-permute-start | bytes 196616 | tf_op jit(solution)/shard_map/ppermute | solution.py:93
  17.9 30.8 %collective-permute-start = (f32[3,1,8,8,256]{4,2,1,0,3:T(8,128)}, f32[3,1,8,8,256]{4,2,1,0,3:T(8,128)}, u32[]{:S(2)}, u32[]{:S(2)}) collective-permute-start(f32[3,1,8,8,256]{4,2,1,0,3:T(8,128)} %slice.588), channel_id=1, source_target_pairs={{0,4},{4,8},{8,12},{12,16},{16,20},{20,24},{24,28},{1,5},{5,9},{9,... | collective-permute-start | bytes 589832 | tf_op jit(solution)/shard_map/ppermute | solution.py:17
  35.2 6.3 %collective-permute-start.6 = (f32[64,256]{1,0:T(8,128)}, f32[64,256]{1,0:T(8,128)S(1)}, u32[]{:S(2)}, u32[]{:S(2)}) collective-permute-start(f32[64,256]{1,0:T(8,128)} %collective-permute-done.4), channel_id=1, source_target_pairs={{0,4},{4,8},{8,12},{12,16},{16,20},{20,24},{24,28},{28,0},{1,5},{5... | collective-permute-start | bytes 196616 | tf_op jit(solution)/shard_map/ppermute | solution.py:88
  41.6 5.9 %collective-permute-start.8 = (f32[64,256]{1,0:T(8,128)S(1)}, f32[64,256]{1,0:T(8,128)S(1)}, u32[]{:S(2)}, u32[]{:S(2)}) collective-permute-start(f32[64,256]{1,0:T(8,128)S(1)} %collective-permute-done.6), channel_id=1, source_target_pairs={{0,4},{4,8},{8,12},{12,16},{16,20},{20,24},{24,28},{28,0},{1,5},{5... | collective-permute-start | bytes 196616 | tf_op jit(solution)/shard_map/ppermute | solution.py:88
  41.6 6.5 %collective-permute-start.9 = (f32[64,256]{1,0:T(8,128)S(1)}, f32[64,256]{1,0:T(8,128)S(1)}, u32[]{:S(2)}, u32[]{:S(2)}) collective-permute-start(f32[64,256]{1,0:T(8,128)S(1)} %collective-permute-done.7), channel_id=1, source_target_pairs={{0,28},{4,0},{8,4},{12,8},{16,12},{20,16},{24,20},{28,24},{1,29},{... | collective-permute-start | bytes 196616 | tf_op jit(solution)/shard_map/ppermute | solution.py:93
  47.5 6.6 %collective-permute-start.10 = (f32[64,256]{1,0:T(8,128)S(1)}, f32[64,256]{1,0:T(8,128)S(1)}, u32[]{:S(2)}, u32[]{:S(2)}) collective-permute-start(f32[64,256]{1,0:T(8,128)S(1)} %collective-permute-done.8), channel_id=1, source_target_pairs={{0,4},{4,8},{8,12},{12,16},{16,20},{20,24},{24,28},{28,0},{1,5},{5... | collective-permute-start | bytes 196616 | tf_op jit(solution)/shard_map/ppermute | solution.py:88
  50.5 7.5 %collective-permute-start.1 = (f32[3,1,8,8,256]{4,2,1,0,3:T(8,128)}, f32[3,1,8,8,256]{4,2,1,0,3:T(8,128)S(1)}, u32[]{:S(2)}, u32[]{:S(2)}) collective-permute-start(f32[3,1,8,8,256]{4,2,1,0,3:T(8,128)} %get-tuple-element.186), channel_id=1, source_target_pairs={{4,0},{8,4},{12,8},{16,12},{20,16},{24,20},{28,24},{5,1},{9,5},{13... | collective-permute-start | bytes 589832 | tf_op jit(solution)/shard_map/ppermute | solution.py:20
  63.1 11.9 %collective-permute-start.2 = (f32[3,10,1,8,256]{4,2,1,0,3:T(1,128)}, f32[3,10,1,8,256]{4,2,1,0,3:T(1,128)}, u32[]{:S(2)}, u32[]{:S(2)}) collective-permute-start(f32[3,10,1,8,256]{4,2,1,0,3:T(1,128)} %get-tuple-element.181), channel_id=1, source_target_pairs={{0,1},{1,2},{2,3},{4,5},{5,6},{6,7},{8,9},{9,10},{10,11},{12,13},{... | collective-permute-start | bytes 737288 | tf_op jit(solution)/shard_map/ppermute | solution.py:17
  72.9 8.9 %collective-permute-start.3 = (f32[3,10,1,8,256]{4,2,1,0,3:T(1,128)}, f32[3,10,1,8,256]{4,2,1,0,3:T(1,128)}, u32[]{:S(2)}, u32[]{:S(2)}) collective-permute-start(f32[3,10,1,8,256]{4,2,1,0,3:T(1,128)} %get-tuple-element.180), channel_id=1, source_target_pairs={{1,0},{2,1},{3,2},{5,4},{6,5},{7,6},{9,8},{10,9},{11,10},{13,12},{... | collective-permute-start | bytes 737288 | tf_op jit(solution)/shard_map/ppermute | solution.py:20
  102.4 11.0 %all-to-all-start = ((f32[8,8,256]{2,1,0:T(8,128)}), f32[8,8,256]{2,1,0:T(8,128)S(1)}, u32[]{:S(2)}, u32[]{:S(2)}) async-start(f32[8,8,256]{2,1,0:T(8,128)} %bitcast.16), calls=%async_computation.1 | async-start | bytes 131072 | tf_op jit(solution)/shard_map/all_to_all | solution.py:110
  107.7 105.9 %reduce-scatter.5.cloned.1.call-start = ((), (), s32[]{:S(2)}) async-start(), calls=%async_computation.5 | async-start | bytes 327680 | tf_op jit(solution)/shard_map/reduce_scatter | solution.py:101
  121.2 19.8 %collective-permute-start.15 = (f32[64,256]{1,0:T(8,128)}, f32[64,256]{1,0:T(8,128)}, u32[]{:S(2)}, u32[]{:S(2)}) collective-permute-start(f32[64,256]{1,0:T(8,128)} %bitcast.122), channel_id=1, source_target_pairs={{0,4},{4,8},{8,12},{12,16},{16,20},{20,24},{24,28},{28,0},{1,5},{5... | collective-permute-start | bytes 196616 | tf_op jit(solution)/shard_map/ppermute | solution.py:88
  121.3 21.2 %collective-permute-start.16 = (f32[64,256]{1,0:T(8,128)}, f32[64,256]{1,0:T(8,128)}, u32[]{:S(2)}, u32[]{:S(2)}) collective-permute-start(f32[64,256]{1,0:T(8,128)} %bitcast.122), channel_id=1, source_target_pairs={{0,28},{4,0},{8,4},{12,8},{16,12},{20,16},{24,20},{28,24},{1,29},{... | collective-permute-start | bytes 196616 | tf_op jit(solution)/shard_map/ppermute | solution.py:93
  136.0 18.0 %collective-permute-start.11 = (f32[3,1,8,8,256]{4,2,1,0,3:T(8,128)S(1)}, f32[3,1,8,8,256]{4,2,1,0,3:T(8,128)S(1)}, u32[]{:S(2)}, u32[]{:S(2)}) collective-permute-start(f32[3,1,8,8,256]{4,2,1,0,3:T(8,128)S(1)} %slice.605), channel_id=1, source_target_pairs={{0,4},{4,8},{8,12},{12,16},{16,20},{20,24},{24,28},{1,5},{5,9},{9,... | collective-permute-start | bytes 589832 | tf_op jit(solution)/shard_map/ppermute | solution.py:17
  141.0 7.2 %collective-permute-start.17 = (f32[64,256]{1,0:T(8,128)}, f32[64,256]{1,0:T(8,128)S(1)}, u32[]{:S(2)}, u32[]{:S(2)}) collective-permute-start(f32[64,256]{1,0:T(8,128)} %collective-permute-done.15), channel_id=1, source_target_pairs={{0,4},{4,8},{8,12},{12,16},{16,20},{20,24},{24,28},{28,0},{1,5},{5... | collective-permute-start | bytes 196616 | tf_op jit(solution)/shard_map/ppermute | solution.py:88
  148.1 12.1 %collective-permute-start.19 = (f32[64,256]{1,0:T(8,128)S(1)}, f32[64,256]{1,0:T(8,128)S(1)}, u32[]{:S(2)}, u32[]{:S(2)}) collective-permute-start(f32[64,256]{1,0:T(8,128)S(1)} %collective-permute-done.17), channel_id=1, source_target_pairs={{0,4},{4,8},{8,12},{12,16},{16,20},{20,24},{24,28},{28,0},{1,5},{5... | collective-permute-start | bytes 196616 | tf_op jit(solution)/shard_map/ppermute | solution.py:88
  148.3 14.7 %collective-permute-start.20 = (f32[64,256]{1,0:T(8,128)S(1)}, f32[64,256]{1,0:T(8,128)S(1)}, u32[]{:S(2)}, u32[]{:S(2)}) collective-permute-start(f32[64,256]{1,0:T(8,128)S(1)} %collective-permute-done.18), channel_id=1, source_target_pairs={{0,28},{4,0},{8,4},{12,8},{16,12},{20,16},{24,20},{28,24},{1,29},{... | collective-permute-start | bytes 196616 | tf_op jit(solution)/shard_map/ppermute | solution.py:93
  157.6 12.5 %collective-permute-start.12 = (f32[3,1,8,8,256]{4,2,1,0,3:T(8,128)}, f32[3,1,8,8,256]{4,2,1,0,3:T(8,128)S(1)}, u32[]{:S(2)}, u32[]{:S(2)}) collective-permute-start(f32[3,1,8,8,256]{4,2,1,0,3:T(8,128)} %get-tuple-element.184), channel_id=1, source_target_pairs={{4,0},{8,4},{12,8},{16,12},{20,16},{24,20},{28,24},{5,1},{9,5},{13... | collective-permute-start | bytes 589832 | tf_op jit(solution)/shard_map/ppermute | solution.py:20
  160.2 5.9 %collective-permute-start.21 = (f32[64,256]{1,0:T(8,128)S(1)}, f32[64,256]{1,0:T(8,128)S(1)}, u32[]{:S(2)}, u32[]{:S(2)}) collective-permute-start(f32[64,256]{1,0:T(8,128)S(1)} %collective-permute-done.19), channel_id=1, source_target_pairs={{0,4},{4,8},{8,12},{12,16},{16,20},{20,24},{24,28},{28,0},{1,5},{5... | collective-permute-start | bytes 196616 | tf_op jit(solution)/shard_map/ppermute | solution.py:88
  175.2 13.5 %collective-permute-start.13 = (f32[3,10,1,8,256]{4,2,1,0,3:T(1,128)}, f32[3,10,1,8,256]{4,2,1,0,3:T(1,128)}, u32[]{:S(2)}, u32[]{:S(2)}) collective-permute-start(f32[3,10,1,8,256]{4,2,1,0,3:T(1,128)} %get-tuple-element.179), channel_id=1, source_target_pairs={{0,1},{1,2},{2,3},{4,5},{5,6},{6,7},{8,9},{9,10},{10,11},{12,13},{... | collective-permute-start | bytes 737288 | tf_op jit(solution)/shard_map/ppermute | solution.py:17
  186.8 8.3 %collective-permute-start.14 = (f32[3,10,1,8,256]{4,2,1,0,3:T(1,128)}, f32[3,10,1,8,256]{4,2,1,0,3:T(1,128)}, u32[]{:S(2)}, u32[]{:S(2)}) collective-permute-start(f32[3,10,1,8,256]{4,2,1,0,3:T(1,128)} %get-tuple-element.178), channel_id=1, source_target_pairs={{1,0},{2,1},{3,2},{5,4},{6,5},{7,6},{9,8},{10,9},{11,10},{13,12},{... | collective-permute-start | bytes 737288 | tf_op jit(solution)/shard_map/ppermute | solution.py:20
  215.2 9.0 %all-to-all-start.1 = ((f32[8,8,256]{2,1,0:T(8,128)}), f32[8,8,256]{2,1,0:T(8,128)S(1)}, u32[]{:S(2)}, u32[]{:S(2)}) async-start(f32[8,8,256]{2,1,0:T(8,128)} %bitcast.26), calls=%async_computation.3 | async-start | bytes 131072 | tf_op jit(solution)/shard_map/all_to_all | solution.py:110
  (15 other events, 136.2 us)
Sparse Core Ops, SparseCore 0:
  73.1 19.3 reduce-scatter.2
  186.9 15.4 reduce-scatter.4
